TPU v7x, 256 devices: a whole 4x4x8 slice. The times are simulated.
256 devices in a mesh: group: 32 (over z, x_lo, core), rep: 8 (over x_hi, y).
Axes of the slice: x: 4 (x_hi: 2, x_lo: 2; x = x_hi * 2 + x_lo), y: 4, z: 8, core: 2. Of those that a mesh axis runs over, the one named last changes fastest.
Arguments:
- queries: bfloat16 [256, 256, 3072], P(('group', 'rep')), may hold values from -46 to 46
- keys: bfloat16 [256, 256, 3072], P(('group', 'rep')), may hold values from -46 to 46
- values: bfloat16 [256, 256, 3072], P(('group', 'rep')), may hold values from -24 to 24
- grad_output: bfloat16 [256, 256, 3072], P(('group', 'rep')), may hold values from -6 to 6
- weight_codes: bfloat16 [3072, 3072], P('group'), may hold values from -4 to 4
- weight_scales: float32 [3072, 12], P('group'), may hold values from 0.006 to 0.06
Outputs:
- grad_queries: bfloat16 [256, 256, 3072], P(('group', 'rep'))
- grad_keys: bfloat16 [256, 256, 3072], P(('group', 'rep'))
- grad_values: bfloat16 [256, 256, 3072], P(('group', 'rep'))
- grad_weight: float32 [3072, 3072], P(('group', 'rep'))
All inputs are finite; a program needn't handle non-finite values.
Results may differ from a plain program's by a relative error of at most 0.029.
Values may be sent and summed in bfloat16 or wider, within the bound.
No kernel may reach another device: no remote copies, remote signals or barrier semaphores. Data moves between devices by JAX's collectives and lax.ppermute only.
A program may use at most 128 MiB of HBM per device.

v0:
```python
import jax
import jax.numpy as jnp
from jax import lax
from jax.sharding import Mesh
from jax.sharding import PartitionSpec as P

HD = 128
GROUP = ("group_0", "group_1", "group_2")
GROUP_REP = ("group_0", "group_1", "group_2", "rep")


def from_everyone(value, axis):
    count = lax.axis_size(axis)
    return lax.all_to_all(
        jnp.broadcast_to(value[None], (count, *value.shape)), axis, 0, 0, tiled=True
    )


def in_order(pieces, dim):
    shape = list(pieces.shape[1:])
    shape[dim] *= pieces.shape[0]
    return jnp.moveaxis(pieces, 0, dim).reshape(shape)


def gather_axes(value, axes, dim):
    far, near = axes
    pieces = from_everyone(from_everyone(value, far), near)
    return in_order(pieces.swapaxes(0, 1).reshape(-1, *value.shape), dim)


def cut_along(value, dim, count):
    before, after = (value.shape[:dim], value.shape[dim + 1 :])
    return jnp.moveaxis(value.reshape(*before, count, -1, *after), dim, 0)


def sent_and_summed(value, axis, dim):
    count = lax.axis_size(axis)
    pieces = lax.all_to_all(cut_along(value, dim, count), axis, 0, 0, tiled=True)
    return jnp.sum(pieces, axis=0)


def sum_in_two_steps(value, axes, dim):
    far, near = axes
    pieces = cut_along(value, dim, lax.axis_size(far))
    nearer = sent_and_summed(pieces, near, dim + 1)
    arrived = lax.all_to_all(nearer, far, split_axis=0, concat_axis=0, tiled=True)
    return arrived.sum(axis=0)


def restore(code_rows, scale_rows):
    row_count = code_rows.shape[0]
    block_count = scale_rows.shape[1]
    spread = (
        code_rows.astype(jnp.float32).reshape(row_count, block_count, -1) * scale_rows[:, :, None]
    )
    return spread.reshape(row_count, -1).astype(jnp.bfloat16)


def forward_image(arrays_in):
    query, keyset, valueset = arrays_in
    seq_len = query.shape[0]
    head_count = query.shape[1] // HD
    query_heads = query.reshape(seq_len, head_count, HD)
    key_heads = keyset.reshape(seq_len, head_count, HD)
    value_heads = valueset.reshape(seq_len, head_count, HD)
    scores = jnp.einsum(
        "qhd,khd->hqk", query_heads, key_heads, preferred_element_type=jnp.float32
    ) * HD ** (-0.5)
    highest = jnp.max(scores, axis=2, keepdims=True)
    exponent = jnp.exp(scores - highest)
    probability = exponent / jnp.sum(exponent, axis=2, keepdims=True)
    weight_half = probability.astype(jnp.bfloat16)
    context = jnp.einsum(
        "hqk,khd->qhd", weight_half, value_heads, preferred_element_type=jnp.float32
    )
    return (probability, context.astype(jnp.bfloat16).reshape(seq_len, -1))


def backward_image(arrays_in):
    query, keyset, valueset, probability, grad_context = arrays_in
    seq_len = query.shape[0]
    head_count = query.shape[1] // HD
    query_heads = query.reshape(seq_len, head_count, HD)
    key_heads = keyset.reshape(seq_len, head_count, HD)
    value_heads = valueset.reshape(seq_len, head_count, HD)
    grad_heads = grad_context.reshape(seq_len, head_count, HD)
    weight_half = probability.astype(jnp.bfloat16)
    grad_value = jnp.einsum(
        "hqk,qhd->khd", weight_half, grad_heads, preferred_element_type=jnp.float32
    )
    dprobs = jnp.einsum("qhd,khd->hqk", grad_heads, value_heads, preferred_element_type=jnp.float32)
    row_delta = jnp.sum(probability * dprobs, axis=2, keepdims=True)
    dscores = (probability * (dprobs - row_delta) * HD ** (-0.5)).astype(jnp.bfloat16)
    grad_query = jnp.einsum("hqk,khd->qhd", dscores, key_heads, preferred_element_type=jnp.float32)
    grad_key = jnp.einsum("hqk,qhd->khd", dscores, query_heads, preferred_element_type=jnp.float32)
    return (
        grad_query.astype(jnp.bfloat16).reshape(seq_len, -1),
        grad_key.astype(jnp.bfloat16).reshape(seq_len, -1),
        grad_value.astype(jnp.bfloat16).reshape(seq_len, -1),
    )


def per_device(queries, keys, values, grad_output, weight_codes, weight_scales):
    image_count, seq_len, row_total = queries.shape
    feature_count = grad_output.shape[2]
    local_rows = image_count * seq_len
    probability, contexts = lax.map(forward_image, (queries, keys, values))
    context_flat = contexts.reshape(local_rows, row_total)
    output_flat = grad_output.reshape(local_rows, feature_count)
    group_count = lax.axis_size(GROUP)
    replica_count = lax.axis_size("rep")
    slab_rows = row_total // (group_count * replica_count)
    first_row = lax.axis_index("rep") * slab_rows
    codes_part = lax.dynamic_slice_in_dim(weight_codes, first_row, slab_rows, 0)
    scales_part = lax.dynamic_slice_in_dim(weight_scales, first_row, slab_rows, 0)
    all_output = lax.all_gather(output_flat, "rep", axis=0, tiled=True)
    split_context = jnp.moveaxis(
        context_flat.reshape(local_rows, group_count, replica_count, slab_rows), 2, 0
    )
    split_context = split_context.reshape(replica_count, local_rows, group_count * slab_rows)
    gathered_ctx = lax.all_to_all(split_context, "rep", split_axis=0, concat_axis=1, tiled=True)
    gathered_ctx = gathered_ctx.reshape(replica_count, local_rows, group_count * slab_rows)
    grad_columns = jnp.dot(
        all_output,
        restore(
            gather_axes(codes_part, (("group_0", "group_1"), "group_2"), 0),
            gather_axes(
                scales_part.astype(jnp.bfloat16), (("group_0", "group_1"), "group_2"), 0
            ).astype(scales_part.dtype),
        ).T,
        preferred_element_type=jnp.float32,
    ).astype(jnp.bfloat16)
    output_blocks = all_output.reshape(replica_count, local_rows, feature_count)
    device_terms = jnp.einsum(
        "rlp,rle->rpe", gathered_ctx, output_blocks, preferred_element_type=jnp.float32
    ).astype(jnp.bfloat16)
    grad_weight = sum_in_two_steps(
        jnp.sum(lax.optimization_barrier(device_terms).astype(jnp.float32), axis=0),
        (("group_0", "group_1"), "group_2"),
        0,
    )
    returned = lax.all_to_all(
        grad_columns.reshape(1, replica_count * local_rows, group_count * slab_rows),
        "rep",
        split_axis=1,
        concat_axis=0,
        tiled=True,
    )
    returned = jnp.moveaxis(
        returned.reshape(replica_count, local_rows, group_count, slab_rows), 0, 2
    )
    grad_context = returned.reshape(image_count, seq_len, row_total)
    grad_queries, grad_keys, grad_values = lax.map(
        backward_image, (queries, keys, values, probability, grad_context)
    )
    return (grad_queries, grad_keys, grad_values, grad_weight)


def solution(mesh):
    split = Mesh(
        mesh.devices.reshape(8, 2, 2, mesh.shape["rep"]), ("group_0", "group_1", "group_2", "rep")
    )
    return jax.shard_map(
        per_device,
        mesh=split,
        in_specs=(
            P(GROUP_REP, None, None),
            P(GROUP_REP, None, None),
            P(GROUP_REP, None, None),
            P(GROUP_REP, None, None),
            P(GROUP, None),
            P(GROUP, None),
        ),
        out_specs=(
            P(GROUP_REP, None, None),
            P(GROUP_REP, None, None),
            P(GROUP_REP, None, None),
            P(GROUP_REP, None),
        ),
        check_vma=False,
    )
```

profile of v0, /device:TPU:4, one launch (start us, length us, event | category | flops | bytes accessed | tf_op | source)
XLA Modules:
  0.0 398.7 jit_solution(12941961424991909647)
XLA Ops:
  7.2 0.0 copy-start
  7.2 0.0 all-gather.3.cloned.1.call-start
  7.2 0.7 all-gather.3.cloned.1.call-update
  7.9 0.9 dynamic-slice_convert_fusion
  8.8 0.6 broadcast_in_dim.52
  9.5 9.2 %all-to-all-start.2 = ((bf16[16,12,12]{1,2,0:T(8,128)(2,1)}), bf16[16,12,12]{1,2,0:T(8,128)(2,1)S(1)}, u32[]{:S(2)}, u32[]{:S(2)}) async-start(bf16[16,12,12]{1,2,0:T(8,128)(2,1)} %broadcast_in_dim.52), calls=%async_computation.2 | async-start | bytes 131072 | tf_op jit(solution)/shard_map/all_to_all | solution.py:14
  18.7 9.0 %all-to-all-done.2 = bf16[16,12,12]{1,2,0:T(8,128)(2,1)S(1)} async-done(((bf16[16,12,12]{1,2,0:T(8,128)(2,1)}), bf16[16,12,12]{1,2,0:T(8,128)(2,1)S(1)}, u32[]{:S(2)}, u32[]{:S(2)}) %all-to-all-start.2) | async-done | bytes 4640 | tf_op jit(solution)/shard_map/all_to_all | solution.py:14
  27.8 0.2 reshape.109
  27.9 3.7 all_to_all.48
  31.6 1.3 broadcast_in_dim.50
  33.0 4.4 %all-to-all-start = ((bf16[16,12,3072]{2,1,0:T(8,128)(2,1)}), bf16[16,12,3072]{2,1,0:T(8,128)(2,1)}, u32[]{:S(2)}, u32[]{:S(2)}) async-start(bf16[16,12,3072]{2,1,0:T(8,128)(2,1)} %broadcast_in_dim.50), calls=%async_computation | async-start | bytes 3145728 | tf_op jit(solution)/shard_map/all_to_all | solution.py:14
  37.4 1.6 copy.148
  39.0 2.6 copy.147
  41.6 1.7 copy.149
  43.3 0.0 copy-start.3
  43.3 7.4 %fusion.43 = (f32[24,256]{1,0:T(8,128)S(1)}, f32[24,256,256]{1,2,0:T(8,128)}) fusion(bf16[256,24,128]{0,2,1:T(8,128)(2,1)} %bitcast.77, bf16[256,24,128]{0,2,1:T(8,128)(2,1)} %bitcast.79), kind=kOutput, calls=%fused_computation.38 | convolution fusion | flops 407372032 | bytes 9461760 | tf_op jit(solution)/shard_map/while/body/eval_jaxpr/sub | solution.py:70
  50.7 4.6 %fusion.33 = bf16[256,24,128]{0,2,1:T(8,128)(2,1)} fusion(bf16[256,24,128]{0,2,1:T(8,128)(2,1)S(1)} %bitcast.72, f32[24,256,256]{1,2,0:T(8,128)} %get-tuple-element.74, f32[24,256]{1,0:T(8,128)S(1)} %get-tuple-element.73), kind=kOutput, calls=%fused_computation.28 | convolution fusion | flops 406585344 | bytes 9461760 | tf_op jit(solution)/shard_map/while/body/eval_jaxpr/hqk,khd->qhd/dot_general | solution.py:73
  55.3 2.4 reshape_reshape.8
  57.6 0.7 copy.135
  58.4 1.5 copy.136
  59.8 0.2 reshape.110
  60.1 0.2 copy.121
  60.2 0.3 reshape.106
  60.5 2.4 mul.32
  63.0 6.1 %copy.122 = f32[384,3072]{1,0:T(8,128)} copy(f32[384,3072]{0,1:T(8,128)} %bitcast.67) | data formatting | bytes 9437184 | tf_op jit(solution)/shard_map/mul | solution.py:54
  69.0 8.3 %all-to-all-done = bf16[16,12,3072]{2,1,0:T(8,128)(2,1)} async-done(((bf16[16,12,3072]{2,1,0:T(8,128)(2,1)}), bf16[16,12,3072]{2,1,0:T(8,128)(2,1)}, u32[]{:S(2)}, u32[]{:S(2)}) %all-to-all-start) | async-done | bytes 1179680 | tf_op jit(solution)/shard_map/all_to_all | solution.py:14
  77.3 2.1 copy.118
  79.4 0.3 broadcast_in_dim.51
  79.7 5.6 %all_to_all.49 = bf16[2,16,12,3072]{3,1,2,0:T(8,128)(2,1)S(1)} all-to-all(bf16[2,16,12,3072]{3,1,2,0:T(8,128)(2,1)S(1)} %broadcast_in_dim.51), channel_id=1, replica_groups=mesh['group_0'=8,'group_1'=2,'group_2'=2,'rep'=8] {'group_2'}, dimensions={0} | all-to-all | bytes 4718592 | tf_op jit(solution)/shard_map/all_to_all | solution.py:14
  85.3 8.0 %all-to-all-start.5 = ((bf16[8,256,384]{1,2,0:T(8,128)(2,1)}), bf16[8,256,384]{1,2,0:T(8,128)(2,1)}, u32[]{:S(2)}, u32[]{:S(2)}) async-start(bf16[8,256,384]{1,2,0:T(8,128)(2,1)} %copy.136), calls=%async_computation.5 | async-start | bytes 3145728 | tf_op jit(solution)/shard_map/all_to_all | solution.py:121
  93.3 0.6 convert_bitcast_fusion
  93.8 5.5 %copy.119 = f32[16,2,12,3072]{3,2,1,0:T(8,128)} copy(f32[16,2,12,3072]{3,0,2,1:T(8,128)S(1)} %convert_bitcast_fusion) | data formatting | bytes 9437184 | tf_op jit(solution)/shard_map/convert_element_type | solution.py:54
  99.3 5.4 %reshape.105 = f32[384,3072]{1,0:T(8,128)} reshape(f32[16,2,12,3072]{3,2,1,0:T(8,128)} %copy.119) | data formatting | bytes 9437184 | tf_op jit(solution)/shard_map/convert_element_type | solution.py:54
  104.8 77.1 %all-gather.3.cloned.1.call-done = bf16[1,2048,3072]{2,1,0:T(8,128)(2,1)} async-done(((bf16[1,256,3072]{2,1,0:T(8,128)(2,1)}), bf16[1,2048,3072]{2,1,0:T(8,128)(2,1)}) %all-gather.3.cloned.1.call-update) | async-done | bytes 12582928 | tf_op jit(solution)/shard_map/all_gather | solution.py:116
  181.9 10.8 %fusion.22 = bf16[1,2048,384]{1,2,0:T(8,128)(2,1)S(1)} fusion(bf16[1,2048,3072]{2,1,0:T(8,128)(2,1)} %all-gather.3.cloned.1.call-done, f32[384,3072]{1,0:T(8,128)} %reshape.105, f32[384,3072]{1,0:T(8,128)} %copy.122), kind=kOutput, calls=%fused_computation.21 | convolution fusion | flops 4834983936 | bytes 23592960 | tf_op jit(solution)/shard_map/dot_general | solution.py:123
  192.7 5.6 %copy.123 = bf16[1,2048,384]{2,0,1:T(2,128)(2,1)} copy(bf16[1,2048,384]{1,2,0:T(8,128)(2,1)S(1)} %fusion.22) | data formatting | bytes 3145728 | tf_op jit(solution)/shard_map/reshape | solution.py:143
  198.3 0.5 broadcast.35
  198.9 34.3 %reduce = bf16[2048,384]{1,0:T(8,128)(2,1)S(1)} reduce(bf16[2048,1,384]{2,1,0:T(2,128)(2,1)} %bitcast.68, bf16[]{:T(256)} %broadcast.35), dimensions={1}, to_apply=%bitcast.50.reduce_sub_computation | reduce | bytes 3145730
  233.2 1.9 reshape.111
  235.0 0.0 all-to-all-done.5
  235.0 14.1 %convolution_convert_fusion = bf16[8,384,3072]{2,1,0:T(8,128)(2,1)} fusion(bf16[8,256,384]{1,2,0:T(8,128)(2,1)} %all-to-all-done.5, bf16[8,256,3072]{2,1,0:T(8,128)(2,1)} %bitcast.70), kind=kOutput, calls=%fused_computation.5 | convolution fusion | flops 4841275392 | bytes 33030144 | tf_op jit(solution)/shard_map/rlp,rle->rpe/dot_general | solution.py:134
  249.1 12.8 %convert_reduce_fusion = f32[384,3072]{1,0:T(8,128)} fusion(bf16[8,384,3072]{2,1,0:T(8,128)(2,1)} %convolution_convert_fusion), kind=kLoop, calls=%fused_computation.2 | loop fusion | flops 17694720 | bytes 23592960 | tf_op jit(solution)/shard_map/reduce_sum | solution.py:138
  261.9 5.5 %reshape_reshape.9 = f32[16,2,12,3072]{3,2,1,0:T(8,128)} reshape(f32[384,3072]{1,0:T(8,128)} %convert_reduce_fusion) | data formatting | bytes 9437184 | tf_op jit(solution)/shard_map/reshape;reshape | solution.py:33
  267.4 5.5 %copy.137 = f32[2,16,12,3072]{3,1,2,0:T(8,128)S(1)} copy(f32[2,16,12,3072]{3,2,0,1:T(8,128)} %bitcast.66) | data formatting | bytes 9437184 | tf_op jit(solution)/shard_map/transpose | solution.py:33
  272.9 8.6 %all_to_all.50 = f32[2,16,12,3072]{3,1,2,0:T(8,128)} all-to-all(f32[2,16,12,3072]{3,1,2,0:T(8,128)S(1)} %copy.137), channel_id=1, replica_groups=mesh['group_0'=8,'group_1'=2,'group_2'=2,'rep'=8] {'group_2'}, dimensions={0} | all-to-all | bytes 9437184 | tf_op jit(solution)/shard_map/all_to_all | solution.py:38
  281.6 6.9 %all-to-all-start.4 = ((bf16[8,2,49152]{2,1,0:T(2,128)(2,1)}), bf16[8,2,49152]{2,1,0:T(2,128)(2,1)}, u32[]{:S(2)}, u32[]{:S(2)}) async-start(bf16[8,2,49152]{2,1,0:T(2,128)(2,1)} %reshape.111), calls=%async_computation.4 | async-start | bytes 3145728 | tf_op jit(solution)/shard_map/all_to_all | solution.py:142
  288.5 2.9 reduce_sum.50
  291.4 3.0 copy.138
  294.4 14.6 %all-to-all-done.4 = bf16[8,2,49152]{2,1,0:T(2,128)(2,1)} async-done(((bf16[8,2,49152]{2,1,0:T(2,128)(2,1)}), bf16[8,2,49152]{2,1,0:T(2,128)(2,1)}, u32[]{:S(2)}, u32[]{:S(2)}) %all-to-all-start.4) | async-done | bytes 1572896 | tf_op jit(solution)/shard_map/all_to_all | solution.py:142
  309.0 6.4 %all-to-all-start.7 = ((f32[16,12,3072]{2,1,0:T(8,128)}), f32[16,12,3072]{2,1,0:T(8,128)}, u32[]{:S(2)}, u32[]{:S(2)}) async-start(f32[16,12,3072]{2,1,0:T(8,128)} %copy.138), calls=%async_computation.7 | async-start | bytes 6291456 | tf_op jit(solution)/shard_map/all_to_all | solution.py:46
  315.5 6.3 %reshape.112 = bf16[2048,1,384]{2,1,0:T(2,128)(2,1)} reshape(bf16[8,2,49152]{2,1,0:T(2,128)(2,1)} %all-to-all-done.4) | data formatting | bytes 3145728
  321.8 6.8 %copy.124 = bf16[1,2048,384]{1,2,0:T(8,128)(2,1)S(1)} copy(bf16[1,2048,384]{2,0,1:T(2,128)(2,1)} %bitcast.69) | data formatting | bytes 3145728 | tf_op jit(solution)/shard_map/all_to_all | solution.py:142
  328.6 0.5 copy.150
  329.1 0.5 copy.125
  329.6 1.3 reshape.101
  331.0 5.6 %convolution_convert_fusion.2 = bf16[24,128,256]{2,1,0:T(8,128)(2,1)} fusion(bf16[256,24,128]{0,2,1:T(8,128)(2,1)} %reshape.101, f32[24,256,256]{1,2,0:T(8,128)} %get-tuple-element.74, f32[24,256]{1,0:T(8,128)S(1)} %get-tuple-element.73), kind=kOutput, calls=%fused_computation.25 | convolution fusion | flops 406585344 | bytes 9461760 | tf_op jit(solution)/shard_map/while/body/eval_jaxpr/hqk,qhd->khd/dot_general | solution.py:88
  336.6 2.7 copy.141
  339.3 5.1 %fusion.44 = f32[24,256,256]{1,2,0:T(8,128)} fusion(bf16[256,24,128]{0,2,1:T(8,128)(2,1)} %bitcast.73, bf16[256,24,128]{0,2,1:T(8,128)(2,1)S(1)} %copy-done.2), kind=kOutput, calls=%fused_computation.40 | convolution fusion | flops 402653184 | bytes 9437184 | tf_op jit(solution)/shard_map/while/body/eval_jaxpr/qhd,khd->hqk/dot_general | solution.py:91
  344.3 12.2 %fusion.25 = bf16[24,256,128]{1,2,0:T(8,128)(2,1)} fusion(bf16[256,24,128]{0,2,1:T(8,128)(2,1)} %bitcast.80, f32[24,256,256]{1,2,0:T(8,128)} %fusion.44, f32[24,256,256]{1,2,0:T(8,128)} %get-tuple-element.74, f32[24,256]{1,0:T(8,128)S(1)} %get-tuple-element.73), kind=kOutput, calls=%fused_computation.22 | convolution fusion | flops 414456064 | bytes 15753216 | tf_op jit(solution)/shard_map/while/body/eval_jaxpr/hqk,khd->qhd/dot_general | solution.py:94
  356.5 2.7 copy.139
  359.2 11.9 %fusion.28 = bf16[24,256,128]{1,2,0:T(8,128)(2,1)} fusion(bf16[256,24,128]{0,2,1:T(8,128)(2,1)S(1)} %bitcast.78, f32[24,256,256]{1,2,0:T(8,128)} %fusion.44, f32[24,256,256]{1,2,0:T(8,128)} %get-tuple-element.74, f32[24,256]{1,0:T(8,128)S(1)} %get-tuple-element.73), kind=kOutput, calls=%fused_computation.23 | convolution fusion | flops 414456064 | bytes 15753216 | tf_op jit(solution)/shard_map/while/body/eval_jaxpr/hqk,qhd->khd/dot_general | solution.py:95
  371.1 2.6 copy.140
  373.8 15.1 %all-to-all-done.7 = f32[16,12,3072]{2,1,0:T(8,128)} async-done(((f32[16,12,3072]{2,1,0:T(8,128)}), f32[16,12,3072]{2,1,0:T(8,128)}, u32[]{:S(2)}, u32[]{:S(2)}) %all-to-all-start.7) | async-done | bytes 2359328 | tf_op jit(solution)/shard_map/all_to_all | solution.py:46
  388.8 2.8 reduce_sum.51
  (14 shorter events, 0.1 us)
Async XLA Ops:
  7.2 11.5 %copy-start = (bf16[96,3072]{1,0:T(8,128)(2,1)S(1)}, bf16[96,3072]{1,0:T(8,128)(2,1)}, u32[]{:S(2)}) copy-start(bf16[96,3072]{1,0:T(8,128)(2,1)} %param.10) | copy-start | bytes 1769476
  7.2 174.7 %all-gather.3.cloned.1.call-start = ((), (), s32[]{:S(2)}) async-start(), calls=%async_computation.8 | async-start | bytes 14155776 | tf_op jit(solution)/shard_map/all_gather | solution.py:116
  7.9 29.5 %copy-start.4 = (bf16[1,256,3072]{2,1,0:T(8,128)(2,1)S(1)}, bf16[1,256,3072]{2,1,0:T(8,128)(2,1)}, u32[]{:S(2)}) copy-start(bf16[1,256,3072]{2,1,0:T(8,128)(2,1)} %param.6) | copy-start | bytes 4718596
  9.5 18.3 %all-to-all-start.2 = ((bf16[16,12,12]{1,2,0:T(8,128)(2,1)}), bf16[16,12,12]{1,2,0:T(8,128)(2,1)S(1)}, u32[]{:S(2)}, u32[]{:S(2)}) async-start(bf16[16,12,12]{1,2,0:T(8,128)(2,1)} %broadcast_in_dim.52), calls=%async_computation.2 | async-start | bytes 131072 | tf_op jit(solution)/shard_map/all_to_all | solution.py:14
  33.0 44.4 %all-to-all-start = ((bf16[16,12,3072]{2,1,0:T(8,128)(2,1)}), bf16[16,12,3072]{2,1,0:T(8,128)(2,1)}, u32[]{:S(2)}, u32[]{:S(2)}) async-start(bf16[16,12,3072]{2,1,0:T(8,128)(2,1)} %broadcast_in_dim.50), calls=%async_computation | async-start | bytes 3145728 | tf_op jit(solution)/shard_map/all_to_all | solution.py:14
  43.3 7.4 %copy-start.3 = (bf16[1,256,3072]{1,2,0:T(8,128)(2,1)}, bf16[1,256,3072]{1,2,0:T(8,128)(2,1)S(1)}, u32[]{:S(2)}) copy-start(bf16[1,256,3072]{1,2,0:T(8,128)(2,1)S(1)} %copy.149) | copy-start | bytes 4718596
  85.3 149.7 %all-to-all-start.5 = ((bf16[8,256,384]{1,2,0:T(8,128)(2,1)}), bf16[8,256,384]{1,2,0:T(8,128)(2,1)}, u32[]{:S(2)}, u32[]{:S(2)}) async-start(bf16[8,256,384]{1,2,0:T(8,128)(2,1)} %copy.136), calls=%async_computation.5 | async-start | bytes 3145728 | tf_op jit(solution)/shard_map/all_to_all | solution.py:121
  281.6 27.5 %all-to-all-start.4 = ((bf16[8,2,49152]{2,1,0:T(2,128)(2,1)}), bf16[8,2,49152]{2,1,0:T(2,128)(2,1)}, u32[]{:S(2)}, u32[]{:S(2)}) async-start(bf16[8,2,49152]{2,1,0:T(2,128)(2,1)} %reshape.111), calls=%async_computation.4 | async-start | bytes 3145728 | tf_op jit(solution)/shard_map/all_to_all | solution.py:142
  309.0 79.8 %all-to-all-start.7 = ((f32[16,12,3072]{2,1,0:T(8,128)}), f32[16,12,3072]{2,1,0:T(8,128)}, u32[]{:S(2)}, u32[]{:S(2)}) async-start(f32[16,12,3072]{2,1,0:T(8,128)} %copy.138), calls=%async_computation.7 | async-start | bytes 6291456 | tf_op jit(solution)/shard_map/all_to_all | solution.py:46
  336.6 2.7 copy-start.2
  356.5 2.7 copy-start.5
  371.1 20.5 %copy-start.1 = (bf16[96,3072]{1,0:T(8,128)(2,1)S(1)}, bf16[96,3072]{1,0:T(8,128)(2,1)}, u32[]{:S(2)}) copy-start(bf16[96,3072]{1,0:T(8,128)(2,1)} %param.10) | copy-start | bytes 1769476
Sparse Core Ops, SparseCore 0:
  10.6 171.2 all-gather.2
where the time goes:
time: 406 us; the launch traced here: 399 us
  waiting for transfers between devices  125 us (31%)
  local copies, waits for them, and re-layouts  81.5 us (20%)
  matrix products  71.7 us (18%)
  other arithmetic  53.3 us (13%)
  starting transfers between devices  35 us (9%)
  blocking collectives  18 us (4%)
  between operations  14.5 us (4%)
    all_gather x1, waiting for transfers between devices, per_device(): all_output = lax.all_gather(output_flat, 'rep', axis=0, tiled=True)  77.1 us
    unnamed x1, other arithmetic  34.3 us
    unnamed x22, local copies, waits for them, and re-layouts  17.7 us
    all_to_all x2, waiting for transfers between devices, from_everyone(): lax.all_to_all(jnp.broadcast_to(value[None], (count, *value.shape)), axis...  17.3 us
    all_to_all x1, waiting for transfers between devices, sum_in_two_steps(): lax.all_to_all(nearer, far, split_axis=0, concat_axis=0, tiled=True)  15.1 us
    all_to_all x1, waiting for transfers between devices, per_device(): lax.all_to_all(grad_columns.reshape(1, replica_count * local_rows, group_...  14.6 us
    dot_general x1, matrix products, per_device(): jnp.einsum('rlp,rle->rpe', gathered_ctx, output_blocks, preferred_element...  14.1 us
    all_to_all x2, starting transfers between devices, from_everyone(): lax.all_to_all(jnp.broadcast_to(value[None], (count, *value.shape)), axis...  13.6 us
  transfers between devices with their start and end apart: 6, of which 5 were waited for; matrix products, arithmetic and copies ran while one was open for 42% of the time, Pallas kernels for 0%

commit v1 on v0

--- a/solution.py
+++ b/solution.py
@@ -139,12 +139,21 @@
         (("group_0", "group_1"), "group_2"),
         0,
     )
-    returned = lax.all_to_all(
-        grad_columns.reshape(1, replica_count * local_rows, group_count * slab_rows),
-        "rep",
-        split_axis=1,
-        concat_axis=0,
-        tiled=True,
+    returned = jnp.concatenate(
+        lax.all_to_all(
+            jnp.stack(
+                jnp.split(
+                    grad_columns.reshape(1, replica_count * local_rows, group_count * slab_rows),
+                    lax.axis_size("rep"),
+                    axis=1,
+                ),
+                axis=0,
+            ),
+            "rep",
+            split_axis=0,
+            concat_axis=0,
+        ),
+        axis=0,
     )
     returned = jnp.moveaxis(
         returned.reshape(replica_count, local_rows, group_count, slab_rows), 0, 2

time: 406 us -> 363 us (0.89); the launches traced: 399 us -> 361 us
  other arithmetic: 53.3 us -> 19 us
  local copies, waits for them, and re-layouts: 81.5 us -> 67.7 us
  waiting for transfers between devices: 125 us -> 137 us
    unnamed x1 -> x0, other arithmetic: 34.3 us -> none
    all_to_all x1, waiting for transfers between devices: 15.1 us -> 26.4 us  [sum_in_two_steps(): lax.all_to_all(nearer, far, split_axis=0, concat_axis=0, tiled=True)]
    reshape x1 -> x0, local copies, waits for them, and re-layouts: 5.62 us -> none  [per_device(): grad_columns.reshape(1, replica_count * local_rows, group_count * slab_rows)]
    all_to_all x1, local copies, waits for them, and re-layouts: 6.77 us -> 2.29 us  [per_device(): lax.all_to_all(jnp.stack(jnp.split(grad_columns.reshape(1, replica_count...]
    unnamed x22 -> x25, local copies, waits for them, and re-layouts: 17.7 us -> 13.4 us
  transfers between devices with their start and end apart: 6 -> 6, of which waited for: 5 -> 5; matrix products, arithmetic and copies ran while one was open for 42% -> 33% of each run, Pallas kernels for 0% -> 0%
where the time goes in v1:
time: 363 us; the launch traced here: 361 us
  waiting for transfers between devices  137 us (38%)
  matrix products  71.5 us (20%)
  local copies, waits for them, and re-layouts  67.7 us (19%)
  starting transfers between devices  34.3 us (9%)
  other arithmetic  19 us (5%)
  blocking collectives  18 us (5%)
  between operations  14.2 us (4%)
    all_gather x1, waiting for transfers between devices, per_device(): all_output = lax.all_gather(output_flat, 'rep', axis=0, tiled=True)  77.7 us
    all_to_all x1, waiting for transfers between devices, sum_in_two_steps(): lax.all_to_all(nearer, far, split_axis=0, concat_axis=0, tiled=True)  26.4 us
    all_to_all x2, waiting for transfers between devices, from_everyone(): lax.all_to_all(jnp.broadcast_to(value[None], (count, *value.shape)), axis...  17.3 us
    all_to_all x1, waiting for transfers between devices, per_device(): lax.all_to_all(jnp.stack(jnp.split(grad_columns.reshape(1, replica_count...  14.6 us
    dot_general x1, matrix products, per_device(): jnp.einsum('rlp,rle->rpe', gathered_ctx, output_blocks, preferred_element...  13.9 us
    all_to_all x2, starting transfers between devices, from_everyone(): lax.all_to_all(jnp.broadcast_to(value[None], (count, *value.shape)), axis...  13.6 us
    unnamed x25, local copies, waits for them, and re-layouts  13.4 us
    reduce_sum x1, other arithmetic, per_device(): jnp.sum(lax.optimization_barrier(device_terms).astype(jnp.float32), axis=0)  12.8 us
  transfers between devices with their start and end apart: 6, of which 5 were waited for; matrix products, arithmetic and copies ran while one was open for 33% of the time, Pallas kernels for 0%

profile of v1, /device:TPU:4, one launch (start us, length us, event | category | flops | bytes accessed | tf_op | source)
XLA Modules:
  0.0 361.4 jit_solution(6261090021535119067)
XLA Ops:
  7.2 0.0 copy-start
  7.2 0.0 all-gather.3.cloned.1.call-start
  7.2 0.7 all-gather.3.cloned.1.call-update
  7.9 0.8 dynamic-slice_convert_fusion
  8.7 0.6 broadcast_in_dim.52
  9.3 9.2 %all-to-all-start.2 = ((bf16[16,12,12]{1,2,0:T(8,128)(2,1)}), bf16[16,12,12]{1,2,0:T(8,128)(2,1)S(1)}, u32[]{:S(2)}, u32[]{:S(2)}) async-start(bf16[16,12,12]{1,2,0:T(8,128)(2,1)} %broadcast_in_dim.52), calls=%async_computation.2 | async-start | bytes 131072 | tf_op jit(solution)/shard_map/all_to_all | solution.py:14
  18.6 9.0 %all-to-all-done.2 = bf16[16,12,12]{1,2,0:T(8,128)(2,1)S(1)} async-done(((bf16[16,12,12]{1,2,0:T(8,128)(2,1)}), bf16[16,12,12]{1,2,0:T(8,128)(2,1)S(1)}, u32[]{:S(2)}, u32[]{:S(2)}) %all-to-all-start.2) | async-done | bytes 4640 | tf_op jit(solution)/shard_map/all_to_all | solution.py:14
  27.6 0.2 reshape.101
  27.8 3.7 %all_to_all.44 = bf16[2,2,1152]{2,1,0:T(2,128)(2,1)S(1)} all-to-all(bf16[2,2,1152]{2,1,0:T(2,128)(2,1)S(1)} %reshape.101), channel_id=1, replica_groups=mesh['group_0'=8,'group_1'=2,'group_2'=2,'rep'=8] {'group_2'}, dimensions={0} | all-to-all | bytes 18432 | tf_op jit(solution)/shard_map/all_to_all | solution.py:14
  31.5 1.3 broadcast_in_dim.50
  32.8 4.4 %all-to-all-start = ((bf16[16,12,3072]{2,1,0:T(8,128)(2,1)}), bf16[16,12,3072]{2,1,0:T(8,128)(2,1)}, u32[]{:S(2)}, u32[]{:S(2)}) async-start(bf16[16,12,3072]{2,1,0:T(8,128)(2,1)} %broadcast_in_dim.50), calls=%async_computation | async-start | bytes 3145728 | tf_op jit(solution)/shard_map/all_to_all | solution.py:14
  37.3 1.6 copy.123
  38.9 2.6 copy.122
  41.5 1.7 copy.124
  43.2 7.4 %fusion.51 = (f32[24,256]{1,0:T(8,128)S(1)}, f32[24,256,256]{1,2,0:T(8,128)}) fusion(bf16[256,24,128]{0,2,1:T(8,128)(2,1)} %bitcast.99, bf16[256,24,128]{0,2,1:T(8,128)(2,1)} %bitcast.101), kind=kOutput, calls=%fused_computation.54 | convolution fusion | flops 407372032 | bytes 9461760 | tf_op jit(solution)/shard_map/while/body/eval_jaxpr/sub | solution.py:70
  50.6 4.6 %fusion.33 = bf16[256,24,128]{0,2,1:T(8,128)(2,1)} fusion(bf16[256,24,128]{0,2,1:T(8,128)(2,1)S(1)} %bitcast.95, f32[24,256,256]{1,2,0:T(8,128)} %get-tuple-element.70, f32[24,256]{1,0:T(8,128)S(1)} %get-tuple-element.69), kind=kOutput, calls=%fused_computation.28 | convolution fusion | flops 406585344 | bytes 9461760 | tf_op jit(solution)/shard_map/while/body/eval_jaxpr/hqk,khd->qhd/dot_general | solution.py:73
  55.2 2.4 reshape_reshape.12
  57.5 0.7 copy.110
  58.2 1.5 copy.111
  59.7 0.2 reshape.102
  60.0 0.2 copy.97
  60.1 0.3 reshape.98
  60.4 2.4 mul.32
  62.8 6.1 %copy.98 = f32[384,3072]{1,0:T(8,128)} copy(f32[384,3072]{0,1:T(8,128)} %bitcast.92) | data formatting | bytes 9437184 | tf_op jit(solution)/shard_map/mul | solution.py:54
  68.9 8.3 %all-to-all-done = bf16[16,12,3072]{2,1,0:T(8,128)(2,1)} async-done(((bf16[16,12,3072]{2,1,0:T(8,128)(2,1)}), bf16[16,12,3072]{2,1,0:T(8,128)(2,1)}, u32[]{:S(2)}, u32[]{:S(2)}) %all-to-all-start) | async-done | bytes 1179680 | tf_op jit(solution)/shard_map/all_to_all | solution.py:14
  77.2 2.1 copy.94
  79.3 0.3 broadcast_in_dim.51
  79.6 5.6 %all_to_all.45 = bf16[2,16,12,3072]{3,1,2,0:T(8,128)(2,1)S(1)} all-to-all(bf16[2,16,12,3072]{3,1,2,0:T(8,128)(2,1)S(1)} %broadcast_in_dim.51), channel_id=1, replica_groups=mesh['group_0'=8,'group_1'=2,'group_2'=2,'rep'=8] {'group_2'}, dimensions={0} | all-to-all | bytes 4718592 | tf_op jit(solution)/shard_map/all_to_all | solution.py:14
  85.2 7.4 %all-to-all-start.5 = ((bf16[8,256,384]{1,2,0:T(8,128)(2,1)}), bf16[8,256,384]{1,2,0:T(8,128)(2,1)}, u32[]{:S(2)}, u32[]{:S(2)}) async-start(bf16[8,256,384]{1,2,0:T(8,128)(2,1)} %copy.111), calls=%async_computation.5 | async-start | bytes 3145728 | tf_op jit(solution)/shard_map/all_to_all | solution.py:121
  92.6 0.6 convert_bitcast_fusion
  93.2 5.5 %copy.95 = f32[16,2,12,3072]{3,2,1,0:T(8,128)} copy(f32[16,2,12,3072]{3,0,2,1:T(8,128)S(1)} %convert_bitcast_fusion) | data formatting | bytes 9437184 | tf_op jit(solution)/shard_map/convert_element_type | solution.py:54
  98.7 5.4 %reshape.97 = f32[384,3072]{1,0:T(8,128)} reshape(f32[16,2,12,3072]{3,2,1,0:T(8,128)} %copy.95) | data formatting | bytes 9437184 | tf_op jit(solution)/shard_map/convert_element_type | solution.py:54
  104.1 77.7 %all-gather.3.cloned.1.call-done = bf16[1,2048,3072]{2,1,0:T(8,128)(2,1)} async-done(((bf16[1,256,3072]{2,1,0:T(8,128)(2,1)}), bf16[1,2048,3072]{2,1,0:T(8,128)(2,1)}) %all-gather.3.cloned.1.call-update) | async-done | bytes 12582928 | tf_op jit(solution)/shard_map/all_gather | solution.py:116
  181.8 10.8 %fusion.22 = bf16[1,2048,384]{1,2,0:T(8,128)(2,1)S(1)} fusion(bf16[1,2048,3072]{2,1,0:T(8,128)(2,1)} %all-gather.3.cloned.1.call-done, f32[384,3072]{1,0:T(8,128)} %reshape.97, f32[384,3072]{1,0:T(8,128)} %copy.98), kind=kOutput, calls=%fused_computation.21 | convolution fusion | flops 4834983936 | bytes 23592960 | tf_op jit(solution)/shard_map/dot_general | solution.py:123
  192.6 0.7 fusion.45
  193.3 0.7 fusion.44
  194.0 0.7 fusion.43
  194.7 0.7 fusion.42
  195.4 0.7 fusion.41
  196.1 0.7 fusion.40
  196.8 0.7 fusion.39
  197.5 0.7 fusion.38
  198.2 13.9 %convolution_convert_fusion = bf16[8,384,3072]{2,1,0:T(8,128)(2,1)} fusion(bf16[8,256,384]{1,2,0:T(8,128)(2,1)} %all-to-all-done.5, bf16[8,256,3072]{2,1,0:T(8,128)(2,1)} %bitcast.93), kind=kOutput, calls=%fused_computation.5 | convolution fusion | flops 4841275392 | bytes 33030144 | tf_op jit(solution)/shard_map/rlp,rle->rpe/dot_general | solution.py:134
  212.2 12.8 %convert_reduce_fusion = f32[384,3072]{1,0:T(8,128)} fusion(bf16[8,384,3072]{2,1,0:T(8,128)(2,1)} %convolution_convert_fusion), kind=kLoop, calls=%fused_computation.2 | loop fusion | flops 17694720 | bytes 23592960 | tf_op jit(solution)/shard_map/reduce_sum | solution.py:138
  224.9 5.5 %reshape_reshape.13 = f32[16,2,12,3072]{3,2,1,0:T(8,128)} reshape(f32[384,3072]{1,0:T(8,128)} %convert_reduce_fusion) | data formatting | bytes 9437184 | tf_op jit(solution)/shard_map/reshape;reshape | solution.py:33
  230.5 5.5 %copy.112 = f32[2,16,12,3072]{3,1,2,0:T(8,128)S(1)} copy(f32[2,16,12,3072]{3,2,0,1:T(8,128)} %bitcast.91) | data formatting | bytes 9437184 | tf_op jit(solution)/shard_map/transpose | solution.py:33
  236.0 8.6 %all_to_all.46 = f32[2,16,12,3072]{3,1,2,0:T(8,128)} all-to-all(f32[2,16,12,3072]{3,1,2,0:T(8,128)S(1)} %copy.112), channel_id=1, replica_groups=mesh['group_0'=8,'group_1'=2,'group_2'=2,'rep'=8] {'group_2'}, dimensions={0} | all-to-all | bytes 9437184 | tf_op jit(solution)/shard_map/all_to_all | solution.py:38
  244.6 6.9 %all-to-all-start.4 = ((bf16[8,1,256,384]{2,3,1,0:T(8,128)(2,1)}), bf16[8,1,256,384]{2,3,1,0:T(8,128)(2,1)}, u32[]{:S(2)}, u32[]{:S(2)}) async-start(bf16[8,1,256,384]{2,3,1,0:T(8,128)(2,1)} %fusion.38), calls=%async_computation.4 | async-start | bytes 3145728 | tf_op jit(solution)/shard_map/all_to_all | solution.py:143
  251.5 2.9 reduce_sum.50
  254.4 3.0 copy.113
  257.4 14.6 %all-to-all-done.4 = bf16[8,1,256,384]{2,3,1,0:T(8,128)(2,1)} async-done(((bf16[8,1,256,384]{2,3,1,0:T(8,128)(2,1)}), bf16[8,1,256,384]{2,3,1,0:T(8,128)(2,1)}, u32[]{:S(2)}, u32[]{:S(2)}) %all-to-all-start.4) | async-done | bytes 1572896 | tf_op jit(solution)/shard_map/all_to_all | solution.py:143
  272.1 6.4 %all-to-all-start.7 = ((f32[16,12,3072]{2,1,0:T(8,128)}), f32[16,12,3072]{2,1,0:T(8,128)}, u32[]{:S(2)}, u32[]{:S(2)}) async-start(f32[16,12,3072]{2,1,0:T(8,128)} %copy.113), calls=%async_computation.7 | async-start | bytes 6291456 | tf_op jit(solution)/shard_map/all_to_all | solution.py:46
  278.4 2.3 copy.99
  280.7 0.5 copy.100
  281.2 1.3 reshape.93
  282.6 5.6 %convolution_convert_fusion.2 = bf16[24,128,256]{2,1,0:T(8,128)(2,1)} fusion(bf16[256,24,128]{0,2,1:T(8,128)(2,1)} %reshape.93, f32[24,256,256]{1,2,0:T(8,128)} %get-tuple-element.70, f32[24,256]{1,0:T(8,128)S(1)} %get-tuple-element.69), kind=kOutput, calls=%fused_computation.25 | convolution fusion | flops 406585344 | bytes 9461760 | tf_op jit(solution)/shard_map/while/body/eval_jaxpr/hqk,qhd->khd/dot_general | solution.py:88
  288.2 2.7 copy.116
  290.9 5.1 %fusion.52 = f32[24,256,256]{1,2,0:T(8,128)} fusion(bf16[256,24,128]{0,2,1:T(8,128)(2,1)} %bitcast.96, bf16[256,24,128]{0,2,1:T(8,128)(2,1)S(1)} %copy-done.2), kind=kOutput, calls=%fused_computation.56 | convolution fusion | flops 402653184 | bytes 9437184 | tf_op jit(solution)/shard_map/while/body/eval_jaxpr/qhd,khd->hqk/dot_general | solution.py:91
  296.0 12.2 %fusion.25 = bf16[24,256,128]{1,2,0:T(8,128)(2,1)} fusion(bf16[256,24,128]{0,2,1:T(8,128)(2,1)} %bitcast.102, f32[24,256,256]{1,2,0:T(8,128)} %fusion.52, f32[24,256,256]{1,2,0:T(8,128)} %get-tuple-element.70, f32[24,256]{1,0:T(8,128)S(1)} %get-tuple-element.69), kind=kOutput, calls=%fused_computation.22 | convolution fusion | flops 414456064 | bytes 15753216 | tf_op jit(solution)/shard_map/while/body/eval_jaxpr/hqk,khd->qhd/dot_general | solution.py:94
  308.2 2.7 copy.114
  310.9 11.9 %fusion.28 = bf16[24,256,128]{1,2,0:T(8,128)(2,1)} fusion(bf16[256,24,128]{0,2,1:T(8,128)(2,1)S(1)} %bitcast.100, f32[24,256,256]{1,2,0:T(8,128)} %fusion.52, f32[24,256,256]{1,2,0:T(8,128)} %get-tuple-element.70, f32[24,256]{1,0:T(8,128)S(1)} %get-tuple-element.69), kind=kOutput, calls=%fused_computation.23 | convolution fusion | flops 414456064 | bytes 15753216 | tf_op jit(solution)/shard_map/while/body/eval_jaxpr/hqk,qhd->khd/dot_general | solution.py:95
  322.8 2.6 copy.115
  325.4 26.4 %all-to-all-done.7 = f32[16,12,3072]{2,1,0:T(8,128)} async-done(((f32[16,12,3072]{2,1,0:T(8,128)}), f32[16,12,3072]{2,1,0:T(8,128)}, u32[]{:S(2)}, u32[]{:S(2)}) %all-to-all-start.7) | async-done | bytes 2359328 | tf_op jit(solution)/shard_map/all_to_all | solution.py:46
  351.8 2.8 reduce_sum.51
  (16 shorter events, 0.1 us)
Async XLA Ops:
  7.2 11.4 %copy-start = (bf16[96,3072]{1,0:T(8,128)(2,1)S(1)}, bf16[96,3072]{1,0:T(8,128)(2,1)}, u32[]{:S(2)}) copy-start(bf16[96,3072]{1,0:T(8,128)(2,1)} %param.10) | copy-start | bytes 1769476
  7.2 174.6 %all-gather.3.cloned.1.call-start = ((), (), s32[]{:S(2)}) async-start(), calls=%async_computation.8 | async-start | bytes 14155776 | tf_op jit(solution)/shard_map/all_gather | solution.py:116
  9.3 18.3 %all-to-all-start.2 = ((bf16[16,12,12]{1,2,0:T(8,128)(2,1)}), bf16[16,12,12]{1,2,0:T(8,128)(2,1)S(1)}, u32[]{:S(2)}, u32[]{:S(2)}) async-start(bf16[16,12,12]{1,2,0:T(8,128)(2,1)} %broadcast_in_dim.52), calls=%async_computation.2 | async-start | bytes 131072 | tf_op jit(solution)/shard_map/all_to_all | solution.py:14
  31.5 5.7 %copy-start.4 = (bf16[1,256,3072]{2,1,0:T(8,128)(2,1)S(1)}, bf16[1,256,3072]{2,1,0:T(8,128)(2,1)}, u32[]{:S(2)}) copy-start(bf16[1,256,3072]{2,1,0:T(8,128)(2,1)} %param.6) | copy-start | bytes 4718596
  32.8 44.4 %all-to-all-start = ((bf16[16,12,3072]{2,1,0:T(8,128)(2,1)}), bf16[16,12,3072]{2,1,0:T(8,128)(2,1)}, u32[]{:S(2)}, u32[]{:S(2)}) async-start(bf16[16,12,3072]{2,1,0:T(8,128)(2,1)} %broadcast_in_dim.50), calls=%async_computation | async-start | bytes 3145728 | tf_op jit(solution)/shard_map/all_to_all | solution.py:14
  43.2 7.4 %copy-start.3 = (bf16[1,256,3072]{1,2,0:T(8,128)(2,1)}, bf16[1,256,3072]{1,2,0:T(8,128)(2,1)S(1)}, u32[]{:S(2)}) copy-start(bf16[1,256,3072]{1,2,0:T(8,128)(2,1)S(1)} %copy.124) | copy-start | bytes 4718596
  85.2 113.0 %all-to-all-start.5 = ((bf16[8,256,384]{1,2,0:T(8,128)(2,1)}), bf16[8,256,384]{1,2,0:T(8,128)(2,1)}, u32[]{:S(2)}, u32[]{:S(2)}) async-start(bf16[8,256,384]{1,2,0:T(8,128)(2,1)} %copy.111), calls=%async_computation.5 | async-start | bytes 3145728 | tf_op jit(solution)/shard_map/all_to_all | solution.py:121
  244.6 27.5 %all-to-all-start.4 = ((bf16[8,1,256,384]{2,3,1,0:T(8,128)(2,1)}), bf16[8,1,256,384]{2,3,1,0:T(8,128)(2,1)}, u32[]{:S(2)}, u32[]{:S(2)}) async-start(bf16[8,1,256,384]{2,3,1,0:T(8,128)(2,1)} %fusion.38), calls=%async_computation.4 | async-start | bytes 3145728 | tf_op jit(solution)/shard_map/all_to_all | solution.py:143
  272.1 79.7 %all-to-all-start.7 = ((f32[16,12,3072]{2,1,0:T(8,128)}), f32[16,12,3072]{2,1,0:T(8,128)}, u32[]{:S(2)}, u32[]{:S(2)}) async-start(f32[16,12,3072]{2,1,0:T(8,128)} %copy.113), calls=%async_computation.7 | async-start | bytes 6291456 | tf_op jit(solution)/shard_map/all_to_all | solution.py:46
  288.2 2.7 copy-start.2
  308.2 2.7 copy-start.5
  322.7 31.8 %copy-start.1 = (bf16[96,3072]{1,0:T(8,128)(2,1)S(1)}, bf16[96,3072]{1,0:T(8,128)(2,1)}, u32[]{:S(2)}) copy-start(bf16[96,3072]{1,0:T(8,128)(2,1)} %param.10) | copy-start | bytes 1769476
Sparse Core Ops, SparseCore 0:
  10.6 171.1 all-gather.2
